TPU v7x, 32 devices: a whole 2x2x4 slice. The times are simulated.
32 devices in a mesh: row: 16 (over z, x, core), col: 2 (over y).
Axes of the slice: x: 2, y: 2, z: 4, core: 2. Of those that a mesh axis runs over, the one named last changes fastest.
Arguments:
- token_ids: int32 [512], P('col'), may hold values from 0 to 50559, as said below
- table: bfloat16 [50560, 5120], P('row', 'col'), may hold values from -120 to 120
- norm_gain: float32 [5120], replicated, may hold values from 0.5 to 1.5
- w_qkv: bfloat16 [5120, 7168], P('col', 'row'), may hold values from -0.078125 to 0.078125
- w_gate: bfloat16 [5120, 16384], P('col', 'row'), may hold values from -0.078125 to 0.078125
- w_up: bfloat16 [5120, 16384], P('col', 'row'), may hold values from -0.078125 to 0.078125
Outputs:
- qkv_out: bfloat16 [512, 7168], P('col', 'row')
- hidden: bfloat16 [512, 16384], P('col', 'row')
Inputs may be any that keep to these rules, and one draw needn't show every extreme that they name: `token_ids`: most ids of the micro-batch lie in one block of 3160 entries that starts at a multiple of 3160, which block being drawn; the others lie in the other blocks.
All inputs are finite; a program needn't handle non-finite values.
Results may differ from a plain program's by a relative error of at most 0.0058.
Values may be sent and summed in bfloat16 or wider, within the bound.
A program may use at most 128 MiB of HBM per device.

v0:
```python
import math
import jax
import jax.numpy as jnp
from jax import lax
from jax.sharding import PartitionSpec as P

eps = 1e-05


def lookup_partial(every_id, table_tile, vocab_first):
    total_rows = every_id.shape[0]
    block_rows = math.gcd(total_rows, 512)
    columns = vocab_first + lax.broadcasted_iota(jnp.int32, (1, table_tile.shape[0]), 1)

    def one_block(block_ids):
        onehot = (block_ids[:, None] == columns).astype(jnp.bfloat16)
        return jnp.dot(onehot, table_tile, preferred_element_type=jnp.float32).astype(jnp.bfloat16)

    pieces_out = lax.map(one_block, every_id.reshape(total_rows // block_rows, block_rows))
    return pieces_out.reshape(total_rows, table_tile.shape[1])


def body(token_ids, table, norm_gain, w_qkv, w_gate, w_up):
    every_id = lax.all_gather(token_ids, "col", axis=0, tiled=True)
    vocab_rows = table.shape[0]
    partial_value = lookup_partial(every_id, table, lax.axis_index("row") * vocab_rows)
    embedded = lax.psum(partial_value, "row").astype(jnp.float32).astype(jnp.bfloat16)
    token_rows = lax.all_to_all(embedded, "col", split_axis=0, concat_axis=1, tiled=True)
    values = token_rows.astype(jnp.float32)
    factor = lax.rsqrt(jnp.mean(values * values, axis=1, keepdims=True) + eps)
    normed = (values * factor * norm_gain[None, :]).astype(jnp.bfloat16)
    pieces = (
        lax.all_gather(w_qkv, "col", axis=0, tiled=True),
        lax.all_gather(w_gate, "col", axis=0, tiled=True),
        lax.all_gather(w_up, "col", axis=0, tiled=True),
    )
    qkv_total, gate_total, up_total = tuple(
        (jnp.dot(normed, piece, preferred_element_type=jnp.float32) for piece in pieces)
    )
    qkv_out = qkv_total.astype(jnp.bfloat16)
    hidden = (jax.nn.silu(gate_total) * up_total).astype(jnp.bfloat16)
    return (qkv_out, hidden)


def solution(mesh):
    return jax.shard_map(
        body,
        mesh=mesh,
        in_specs=(
            P("col"),
            P("row", "col"),
            P(),
            P("col", "row"),
            P("col", "row"),
            P("col", "row"),
        ),
        out_specs=(P("col", "row"), P("col", "row")),
        check_vma=False,
    )
```

profile of v0, /device:TPU:0, one launch (start us, length us, event | category | flops | bytes accessed | tf_op | source)
XLA Modules:
  0.0 398.8 jit_solution(8804500506668590405)
XLA Ops:
  8.0 0.0 all-reduce.2.cloned.1.call-start
  8.1 5.4 %all-gather = s32[2,1,256]{2,1,0:T(1,128)S(1)} all-gather(s32[1,1,256]{2,1,0:T(1,128)} %bitcast.20), channel_id=1, replica_groups=mesh['row'=16,'col'=2] {'col'}, dimensions={0}, use_global_device_ids=true | all-gather | bytes 3072 | tf_op jit(solution)/shard_map/all_gather | solution.py:24
  13.5 12.5 %fusion.4 = bf16[512,2560]{1,0:T(8,128)(2,1)S(1)} fusion(bf16[3160,2560]{1,0:T(8,128)(2,1)} %param.7, s32[3160]{0:T(1024)S(1)} %iota_add_fusion, s32[512]{0:T(512)S(1)} %bitcast.19), kind=kOutput, calls=%fused_computation.6 | convolution fusion | flops 8286679040 | bytes 18815328 | tf_op jit(solution)/shard_map/while/body/eval_jaxpr/dot_general | solution.py:17
  26.1 2.6 copy.9
  28.6 0.0 all-reduce.2.cloned.1.call-update
  28.6 0.0 all-gather.5.cloned.1.call-start
  28.7 0.5 all-gather.5.cloned.1.call-update
  29.2 0.0 all-gather.7.cloned.1.call-start
  29.3 0.5 all-gather.7.cloned.1.call-update
  29.8 0.0 all-gather.9.cloned.1.call-start
  29.9 0.5 all-gather.9.cloned.1.call-update
  30.4 0.0 copy-start
  30.4 100.8 %all-reduce.2.cloned.1.call-done = bf16[2,256,2560]{1,2,0:T(8,128)(2,1)} async-done(((bf16[2,256,2560]{1,2,0:T(8,128)(2,1)}), bf16[2,256,2560]{1,2,0:T(8,128)(2,1)}) %all-reduce.2.cloned.1.call-update) | async-done | bytes 2621456 | tf_op jit(solution)/shard_map/psum | solution.py:27
  131.2 63.0 %all_to_all.13 = bf16[2,256,2560]{1,2,0:T(8,128)(2,1)S(1)} all-to-all(bf16[2,256,2560]{1,2,0:T(8,128)(2,1)} %all-reduce.2.cloned.1.call-done), channel_id=1, replica_groups=mesh['row'=16,'col'=2] {'col'}, dimensions={0} | all-to-all | bytes 5242880 | tf_op jit(solution)/shard_map/all_to_all | solution.py:28
  194.1 0.7 multiply_reduce_fusion
  194.9 0.0 copy-done
  194.9 2.2 fusion.3
  197.1 0.0 all-gather.5.cloned.1.call-done
  197.1 4.3 %convolution_convert_fusion = bf16[256,448]{0,1:T(8,128)(2,1)} fusion(bf16[5120,448]{0,1:T(8,128)(2,1)} %all-gather.5.cloned.1.call-done, bf16[256,5120]{0,1:T(8,128)(2,1)S(1)} %fusion.3), kind=kOutput, calls=%fused_computation.11 | convolution fusion | flops 1174519808 | bytes 7438336 | tf_op jit(solution)/shard_map/dot_general | solution.py:38
  201.4 51.0 %all-gather.7.cloned.1.call-done = bf16[5120,1024]{1,0:T(8,128)(2,1)} async-done(((bf16[2560,1024]{1,0:T(8,128)(2,1)}), bf16[5120,1024]{1,0:T(8,128)(2,1)}) %all-gather.7.cloned.1.call-update) | async-done | bytes 10485776 | tf_op jit(solution)/shard_map/all_gather | solution.py:34
  252.4 7.8 %fusion.10 = f32[256,1024]{1,0:T(8,128)} fusion(bf16[256,5120]{0,1:T(8,128)(2,1)S(1)} %fusion.3, bf16[5120,1024]{1,0:T(8,128)(2,1)} %all-gather.7.cloned.1.call-done), kind=kOutput, calls=%fused_computation.14 | convolution fusion | flops 2684354560 | bytes 14155776 | tf_op jit(solution)/shard_map/dot_general | solution.py:38
  260.2 123.0 %all-gather.9.cloned.1.call-done = bf16[5120,1024]{1,0:T(8,128)(2,1)} async-done(((bf16[2560,1024]{1,0:T(8,128)(2,1)}), bf16[5120,1024]{1,0:T(8,128)(2,1)}) %all-gather.9.cloned.1.call-update) | async-done | bytes 10485776 | tf_op jit(solution)/shard_map/all_gather | solution.py:35
  383.2 8.0 %fusion.9 = bf16[256,1024]{1,0:T(8,128)(2,1)} fusion(bf16[256,5120]{0,1:T(8,128)(2,1)S(1)} %fusion.3, bf16[5120,1024]{1,0:T(8,128)(2,1)} %all-gather.9.cloned.1.call-done, f32[256,1024]{1,0:T(8,128)} %fusion.10), kind=kOutput, calls=%fused_computation.10 | convolution fusion | flops 2685927424 | bytes 14680064 | tf_op jit(solution)/shard_map/dot_general | solution.py:38
  (2 shorter events, 0.0 us)
Async XLA Ops:
  8.0 123.2 %all-reduce.2.cloned.1.call-start = ((), (), s32[]{:S(2)}) async-start(), calls=%async_computation.1 | async-start | bytes 5242880 | tf_op jit(solution)/shard_map/psum | solution.py:27
  28.6 168.4 %all-gather.5.cloned.1.call-start = ((), (), s32[]{:S(2)}) async-start(), calls=%async_computation.2 | async-start | bytes 6881280 | tf_op jit(solution)/shard_map/all_gather | solution.py:33
  29.2 223.2 %all-gather.7.cloned.1.call-start = ((), (), s32[]{:S(2)}) async-start(), calls=%async_computation.3 | async-start | bytes 15728640 | tf_op jit(solution)/shard_map/all_gather | solution.py:34
  29.8 353.4 %all-gather.9.cloned.1.call-start = ((), (), s32[]{:S(2)}) async-start(), calls=%async_computation.4 | async-start | bytes 15728640 | tf_op jit(solution)/shard_map/all_gather | solution.py:35
  30.4 164.5 %copy-start = (f32[5120]{0:T(1024)S(1)}, f32[5120]{0:T(1024)}, u32[]{:S(2)}) copy-start(f32[5120]{0:T(1024)} %param.8) | copy-start | bytes 61444
Sparse Core Ops, SparseCore 0:
  28.8 102.3 all-reduce.1
Sparse Core Ops, SparseCore 1:
  30.7 62.7 all-gather.4
  94.9 157.4 all-gather.6
  253.8 129.3 all-gather.8
where the time goes:
time: 399 us
  waiting for transfers between devices  276 us (69%)
  blocking collectives  68.4 us (17%)
  matrix products  32.7 us (8%)
  between operations  15.7 us (4%)
    all_gather x1, waiting for transfers between devices, body(): lax.all_gather(w_up, 'col', axis=0, tiled=True)  123 us
    psum x1, waiting for transfers between devices, body(): lax.psum(partial_value, 'row').astype(jnp.float32).astype(jnp.bfloat16)  101 us
    all_to_all x1, blocking collectives, body(): lax.all_to_all(embedded, 'col', split_axis=0, concat_axis=1, tiled=True)  63 us
    all_gather x1, waiting for transfers between devices, body(): lax.all_gather(w_gate, 'col', axis=0, tiled=True)  51 us
    dot_general x3, matrix products, body(): jnp.dot(normed, piece, preferred_element_type=jnp.float32)  20.2 us
    dot_general x1, matrix products, one_block(): jnp.dot(onehot, table_tile, preferred_element_type=jnp.float32)  12.5 us
  transfers between devices with their start and end apart: 4, of which 3 were waited for; matrix products, arithmetic and copies ran while one was open for 4% of the time, Pallas kernels for 0%

commit v1 on v0

--- a/solution.py
+++ b/solution.py
@@ -5,6 +5,31 @@
 from jax.sharding import PartitionSpec as P
 
 eps = 1e-05
+
+
+def scan_screen(z, in_dim):
+    parts_out = list(z.shape[1:])
+    parts_out[in_dim] *= z.shape[0]
+    return jnp.moveaxis(z, 0, in_dim).reshape(parts_out)
+
+
+def put_the_column(inputs, named_axis):
+    part_now, k_now = (jax.lax.psum(1, named_axis), jax.lax.axis_index(named_axis))
+    carry_in, view_out = (inputs[None], 1)
+    while view_out < part_now:
+        reached = jax.lax.ppermute(
+            carry_in, named_axis, [(ii, ii ^ view_out) for ii in range(part_now)]
+        )
+        item_now = k_now & view_out == 0
+        carry_in = jnp.concatenate(
+            [jnp.where(item_now, carry_in, reached), jnp.where(item_now, reached, carry_in)]
+        )
+        view_out *= 2
+    return carry_in
+
+
+def modes_save(block_in, xx, out_dim):
+    return scan_screen(put_the_column(block_in, xx), out_dim)
 
 
 def lookup_partial(every_id, table_tile, vocab_first):
@@ -32,7 +57,7 @@
     pieces = (
         lax.all_gather(w_qkv, "col", axis=0, tiled=True),
         lax.all_gather(w_gate, "col", axis=0, tiled=True),
-        lax.all_gather(w_up, "col", axis=0, tiled=True),
+        modes_save(w_up, "col", 0),
     )
     qkv_total, gate_total, up_total = tuple(
         (jnp.dot(normed, piece, preferred_element_type=jnp.float32) for piece in pieces)

time: 399 us -> 353 us (0.88)
  blocking collectives: 68.4 us -> 5.44 us
  other arithmetic: 2.91 us -> 12.7 us
  starting transfers between devices: 0.16 us -> 6.2 us
  waiting for transfers between devices: 276 us -> 281 us
  matrix products: 32.7 us -> 28.2 us
    all_to_all x0 -> x1, waiting for transfers between devices: none -> 149 us  [body(): lax.all_to_all(embedded, 'col', split_axis=0, concat_axis=1, tiled=True)]
    all_gather x1 -> x0, waiting for transfers between devices: 123 us -> none  [body(): lax.all_gather(w_up, 'col', axis=0, tiled=True)]
    all_to_all x1 -> x0, blocking collectives: 63 us -> none  [body(): lax.all_to_all(embedded, 'col', split_axis=0, concat_axis=1, tiled=True)]
    all_gather x1, waiting for transfers between devices: 51 us -> 31.5 us  [body(): lax.all_gather(w_gate, 'col', axis=0, tiled=True)]
    select_n x0 -> x1, other arithmetic: none -> 8.69 us  [put_the_column(): jnp.where(item_now, carry_in, reached)]
    dot_general x3, matrix products: 20.2 us -> 15.6 us  [body(): jnp.dot(normed, piece, preferred_element_type=jnp.float32)]
    all_to_all x0 -> x1, starting transfers between devices: none -> 4.03 us  [body(): lax.all_to_all(embedded, 'col', split_axis=0, concat_axis=1, tiled=True)]
  transfers between devices with their start and end apart: 4 -> 5, of which waited for: 3 -> 3; matrix products, arithmetic and copies ran while one was open for 4% -> 5% of each run, Pallas kernels for 0% -> 0%
where the time goes in v1:
time: 353 us
  waiting for transfers between devices  281 us (80%)
  matrix products  28.2 us (8%)
  between operations  15.5 us (4%)
  other arithmetic  12.7 us (4%)
  starting transfers between devices  6.2 us (2%)
  blocking collectives  5.44 us (2%)
  local copies, waits for them, and re-layouts  3.96 us (1%)
    all_to_all x1, waiting for transfers between devices, body(): lax.all_to_all(embedded, 'col', split_axis=0, concat_axis=1, tiled=True)  149 us
    psum x1, waiting for transfers between devices, body(): lax.psum(partial_value, 'row').astype(jnp.float32).astype(jnp.bfloat16)  99.4 us
    all_gather x1, waiting for transfers between devices, body(): lax.all_gather(w_gate, 'col', axis=0, tiled=True)  31.5 us
    dot_general x3, matrix products, body(): jnp.dot(normed, piece, preferred_element_type=jnp.float32)  15.6 us
    dot_general x1, matrix products, one_block(): jnp.dot(onehot, table_tile, preferred_element_type=jnp.float32)  12.5 us
    select_n x1, other arithmetic, put_the_column(): jnp.where(item_now, carry_in, reached)  8.69 us
  transfers between devices with their start and end apart: 5, of which 3 were waited for; matrix products, arithmetic and copies ran while one was open for 5% of the time, Pallas kernels for 0%

profile of v1, /device:TPU:0, one launch (start us, length us, event | category | flops | bytes accessed | tf_op | source)
XLA Modules:
  0.0 353.1 jit_solution(15200671035809601756)
XLA Ops:
  8.0 0.0 all-reduce.2.cloned.1.call-start
  8.0 5.4 %all-gather = s32[2,1,256]{2,1,0:T(1,128)S(1)} all-gather(s32[1,1,256]{2,1,0:T(1,128)} %bitcast.37), channel_id=1, replica_groups=mesh['row'=16,'col'=2] {'col'}, dimensions={0}, use_global_device_ids=true | all-gather | bytes 3072 | tf_op jit(solution)/shard_map/all_gather | solution.py:49
  13.5 12.5 %fusion.8 = bf16[512,2560]{1,0:T(8,128)(2,1)S(1)} fusion(bf16[3160,2560]{1,0:T(8,128)(2,1)} %param.7, s32[3160]{0:T(1024)S(1)} %iota_add_fusion, s32[512]{0:T(512)S(1)} %bitcast.36), kind=kOutput, calls=%fused_computation.13 | convolution fusion | flops 8286679040 | bytes 18815328 | tf_op jit(solution)/shard_map/while/body/eval_jaxpr/dot_general | solution.py:42
  26.1 2.7 copy.10
  28.7 0.0 all-reduce.2.cloned.1.call-update
  28.7 0.0 all-gather.4.cloned.1.call-start
  28.8 0.5 all-gather.4.cloned.1.call-update
  29.3 0.0 copy-start.2
  29.3 0.0 all-gather.6.cloned.1.call-start
  29.4 0.5 all-gather.6.cloned.1.call-update
  29.9 2.0 collective-permute-start
  32.0 99.4 %all-reduce.2.cloned.1.call-done = bf16[2,256,2560]{1,2,0:T(8,128)(2,1)} async-done(((bf16[2,256,2560]{1,2,0:T(8,128)(2,1)}), bf16[2,256,2560]{1,2,0:T(8,128)(2,1)}) %all-reduce.2.cloned.1.call-update) | async-done | bytes 2621456 | tf_op jit(solution)/shard_map/psum | solution.py:52
  131.4 4.0 %all-to-all-start = ((bf16[2,256,2560]{1,2,0:T(8,128)(2,1)}), bf16[2,256,2560]{1,2,0:T(8,128)(2,1)S(1)}, u32[]{:S(2)}, u32[]{:S(2)}) async-start(bf16[2,256,2560]{1,2,0:T(8,128)(2,1)} %all-reduce.2.cloned.1.call-done), calls=%async_computation | async-start | bytes 5242880 | tf_op jit(solution)/shard_map/all_to_all | solution.py:53
  135.4 0.0 copy-done.2
  135.5 149.1 %all-to-all-done = bf16[2,256,2560]{1,2,0:T(8,128)(2,1)S(1)} async-done(((bf16[2,256,2560]{1,2,0:T(8,128)(2,1)}), bf16[2,256,2560]{1,2,0:T(8,128)(2,1)S(1)}, u32[]{:S(2)}, u32[]{:S(2)}) %all-to-all-start) | async-done | bytes 2621472 | tf_op jit(solution)/shard_map/all_to_all | solution.py:53
  284.5 0.7 multiply_reduce_fusion
  285.2 3.2 fusion.7
  288.5 0.0 all-gather.4.cloned.1.call-done
  288.5 5.2 %convolution_convert_fusion = bf16[256,448]{0,1:T(8,128)(2,1)} fusion(bf16[5120,448]{0,1:T(8,128)(2,1)} %all-gather.4.cloned.1.call-done, bf16[256,5120]{0,1:T(8,128)(2,1)} %fusion.7), kind=kOutput, calls=%fused_computation.23 | convolution fusion | flops 1174519808 | bytes 7438336 | tf_op jit(solution)/shard_map/dot_general | solution.py:63
  293.7 0.0 collective-permute-done
  293.7 8.7 %broadcast_select_fusion.1 = (bf16[1,2560,1024]{2,1,0:T(8,128)(2,1)}, bf16[1,2560,1024]{2,1,0:T(8,128)(2,1)}) fusion(bf16[1,2560,1024]{2,1,0:T(8,128)(2,1)} %collective-permute-done, pred[]{:T(512)S(6)} %eq.26, bf16[2560,1024]{1,0:T(8,128)(2,1)} %param.11), kind=kLoop, calls=%fused_computation.12 | loop fusion | flops 5242880 | bytes 20971520 | tf_op jit(solution)/shard_map/jit(_where)/select_n | solution.py:25
  302.4 31.5 %all-gather.6.cloned.1.call-done = bf16[5120,1024]{1,0:T(8,128)(2,1)} async-done(((bf16[2560,1024]{1,0:T(8,128)(2,1)}), bf16[5120,1024]{1,0:T(8,128)(2,1)}) %all-gather.6.cloned.1.call-update) | async-done | bytes 10485776 | tf_op jit(solution)/shard_map/all_gather | solution.py:59
  333.9 0.0 copy-start
  333.9 0.0 copy-start.1
  333.9 6.5 %fusion.34 = f32[256,1024]{1,0:T(8,128)S(1)} fusion(bf16[256,5120]{0,1:T(8,128)(2,1)} %fusion.7, bf16[5120,1024]{1,0:T(8,128)(2,1)} %all-gather.6.cloned.1.call-done), kind=kOutput, calls=%fused_computation.27 | convolution fusion | flops 2684354560 | bytes 14155776 | tf_op jit(solution)/shard_map/dot_general | solution.py:63
  340.5 0.0 copy-done
  340.5 1.3 copy-done.1
  341.8 3.9 %fusion.28 = bf16[256,1024]{1,0:T(8,128)(2,1)} fusion(bf16[1,2560,1024]{2,1,0:T(8,128)(2,1)S(1)} %copy-done.1, bf16[1,2560,1024]{2,1,0:T(8,128)(2,1)S(1)} %copy-done, bf16[2,256,2560]{1,2,0:T(8,128)(2,1)S(1)} %all-to-all-done, f32[2,2560]{1,0:T(2,128)S(1)} %mul.56, f32[256]{0:T(256)S(1)} %add_rsqrt_fusion, f32[256,1024]{1,0:T(8,128)S(1)} %fusion.34), kind=kOutput, calls=%fused_computation.22 | convolution fusion | flops 2696413184 | bytes 14701568 | tf_op jit(solution)/shard_map/dot_general | solution.py:63
  (3 shorter events, 0.0 us)
Async XLA Ops:
  8.0 123.4 %all-reduce.2.cloned.1.call-start = ((), (), s32[]{:S(2)}) async-start(), calls=%async_computation.1 | async-start | bytes 5242880 | tf_op jit(solution)/shard_map/psum | solution.py:52
  28.7 259.8 %all-gather.4.cloned.1.call-start = ((), (), s32[]{:S(2)}) async-start(), calls=%async_computation.2 | async-start | bytes 6881280 | tf_op jit(solution)/shard_map/all_gather | solution.py:58
  29.3 106.1 %copy-start.2 = (f32[5120]{0:T(1024)S(1)}, f32[5120]{0:T(1024)}, u32[]{:S(2)}) copy-start(f32[5120]{0:T(1024)} %param.8) | copy-start | bytes 61444
  29.3 304.6 %all-gather.6.cloned.1.call-start = ((), (), s32[]{:S(2)}) async-start(), calls=%async_computation.3 | async-start | bytes 15728640 | tf_op jit(solution)/shard_map/all_gather | solution.py:59
  29.9 263.8 %collective-permute-start = (bf16[1,2560,1024]{2,1,0:T(8,128)(2,1)}, bf16[1,2560,1024]{2,1,0:T(8,128)(2,1)}, u32[]{:S(2)}, u32[]{:S(2)}) collective-permute-start(bf16[1,2560,1024]{2,1,0:T(8,128)(2,1)} %bitcast.34), channel_id=1, source_target_pairs={{0,1},{1,0},{2,3},{3,2},{4,5},{5,4},{6,7},{7,6},{8,9},{9,8},{10,11... | collective-permute-start | bytes 15728648 | tf_op jit(solution)/shard_map/ppermute | solution.py:20
  131.4 153.1 %all-to-all-start = ((bf16[2,256,2560]{1,2,0:T(8,128)(2,1)}), bf16[2,256,2560]{1,2,0:T(8,128)(2,1)S(1)}, u32[]{:S(2)}, u32[]{:S(2)}) async-start(bf16[2,256,2560]{1,2,0:T(8,128)(2,1)} %all-reduce.2.cloned.1.call-done), calls=%async_computation | async-start | bytes 5242880 | tf_op jit(solution)/shard_map/all_to_all | solution.py:53
  333.9 6.6 %copy-start = (bf16[1,2560,1024]{2,1,0:T(8,128)(2,1)S(1)}, bf16[1,2560,1024]{2,1,0:T(8,128)(2,1)}, u32[]{:S(2)}) copy-start(bf16[1,2560,1024]{2,1,0:T(8,128)(2,1)} %get-tuple-element.12) | copy-start | bytes 15728644
  333.9 7.8 %copy-start.1 = (bf16[1,2560,1024]{2,1,0:T(8,128)(2,1)S(1)}, bf16[1,2560,1024]{2,1,0:T(8,128)(2,1)}, u32[]{:S(2)}) copy-start(bf16[1,2560,1024]{2,1,0:T(8,128)(2,1)} %get-tuple-element.13) | copy-start | bytes 15728644
Sparse Core Ops, SparseCore 0:
  28.9 102.4 all-reduce.1
Sparse Core Ops, SparseCore 1:
  30.7 112.0 all-gather.3
  144.2 189.6 all-gather.5

commit v2 on v0

--- a/solution.py
+++ b/solution.py
@@ -5,6 +5,11 @@
 from jax.sharding import PartitionSpec as P
 
 eps = 1e-05
+
+
+def summed_here(array, mesh_axis):
+    terms = lax.all_gather(array, mesh_axis)
+    return jnp.sum(terms, axis=0)
 
 
 def lookup_partial(every_id, table_tile, vocab_first):
@@ -24,7 +29,7 @@
     every_id = lax.all_gather(token_ids, "col", axis=0, tiled=True)
     vocab_rows = table.shape[0]
     partial_value = lookup_partial(every_id, table, lax.axis_index("row") * vocab_rows)
-    embedded = lax.psum(partial_value, "row").astype(jnp.float32).astype(jnp.bfloat16)
+    embedded = summed_here(partial_value, "row").astype(jnp.float32).astype(jnp.bfloat16)
     token_rows = lax.all_to_all(embedded, "col", split_axis=0, concat_axis=1, tiled=True)
     values = token_rows.astype(jnp.float32)
     factor = lax.rsqrt(jnp.mean(values * values, axis=1, keepdims=True) + eps)

time: 399 us -> 604 us (1.51)
  waiting for transfers between devices: 276 us -> 455 us
  other arithmetic: 2.91 us -> 25.8 us
    all_gather x0 -> x1, waiting for transfers between devices: none -> 207 us  [summed_here(): terms = lax.all_gather(array, mesh_axis)]
    psum x1 -> x0, waiting for transfers between devices: 101 us -> none  [body(): lax.psum(partial_value, 'row').astype(jnp.float32).astype(jnp.bfloat16)]
    all_gather x1, waiting for transfers between devices: 51 us -> 122 us  [body(): lax.all_gather(w_gate, 'col', axis=0, tiled=True)]
    reduce_sum x0 -> x1, other arithmetic: none -> 18.3 us  [summed_here(): return jnp.sum(terms, axis=0)]
  transfers between devices with their start and end apart: 4 -> 4, of which waited for: 3 -> 3; matrix products, arithmetic and copies ran while one was open for 4% -> 7% of each run, Pallas kernels for 0% -> 0%
where the time goes in v2:
time: 604 us; the launch traced here: 603 us
  waiting for transfers between devices  455 us (75%)
  blocking collectives  69 us (11%)
  matrix products  33.8 us (6%)
  other arithmetic  25.8 us (4%)
  between operations  13.8 us (2%)
    all_gather x1, waiting for transfers between devices, summed_here(): terms = lax.all_gather(array, mesh_axis)  207 us
    all_gather x1, waiting for transfers between devices, body(): lax.all_gather(w_up, 'col', axis=0, tiled=True)  123 us
    all_gather x1, waiting for transfers between devices, body(): lax.all_gather(w_gate, 'col', axis=0, tiled=True)  122 us
    all_to_all x1, blocking collectives, body(): lax.all_to_all(embedded, 'col', split_axis=0, concat_axis=1, tiled=True)  63.5 us
    dot_general x3, matrix products, body(): jnp.dot(normed, piece, preferred_element_type=jnp.float32)  20.2 us
    reduce_sum x1, other arithmetic, summed_here(): return jnp.sum(terms, axis=0)  18.3 us
    dot_general x1, matrix products, one_block(): jnp.dot(onehot, table_tile, preferred_element_type=jnp.float32)  13.7 us
  transfers between devices with their start and end apart: 4, of which 3 were waited for; matrix products, arithmetic and copies ran while one was open for 7% of the time, Pallas kernels for 0%

profile of v2, /device:TPU:0, one launch (start us, length us, event | category | flops | bytes accessed | tf_op | source)
XLA Modules:
  0.0 603.2 jit_solution(1444126648186632801)
XLA Ops:
  7.2 0.0 all-gather.13.cloned.1.call-start
  7.2 5.4 all-gather.1
  12.7 13.7 %fusion.5 = bf16[512,2560]{1,0:T(8,128)(2,1)} fusion(bf16[3160,2560]{1,0:T(8,128)(2,1)} %param.7, s32[3160]{0:T(1024)S(1)} %iota_add_fusion, s32[512]{0:T(512)S(1)} %bitcast.21), kind=kOutput, calls=%fused_computation.8 | convolution fusion | flops 8286679040 | bytes 18815328 | tf_op jit(solution)/shard_map/while/body/eval_jaxpr/dot_general | solution.py:22
  26.3 0.0 all-gather.13.cloned.1.call-update
  26.4 0.0 all-gather.7.cloned.1.call-start
  26.4 0.7 all-gather.7.cloned.1.call-update
  27.1 0.0 all-gather.9.cloned.1.call-start
  27.2 0.7 all-gather.9.cloned.1.call-update
  27.8 0.0 all-gather.11.cloned.1.call-start
  27.9 0.5 all-gather.11.cloned.1.call-update
  28.4 207.4 %all-gather.13.cloned.1.call-done = bf16[8192,2560]{1,0:T(8,128)(2,1)} async-done(((bf16[512,2560]{1,0:T(8,128)(2,1)}), bf16[8192,2560]{1,0:T(8,128)(2,1)}) %all-gather.13.cloned.1.call-update) | async-done | bytes 41943056 | tf_op jit(solution)/shard_map/all_gather | solution.py:11
  235.8 18.3 %reduce_sum.21 = bf16[512,2560]{1,0:T(8,128)(2,1)} reduce(bf16[16,512,2560]{2,1,0:T(8,128)(2,1)} %bitcast.19, bf16[]{:T(256)} %constant.16.clone.1), dimensions={0}, to_apply=%region_0.1 | reduce | flops 19660800 | bytes 44564480 | tf_op jit(solution)/shard_map/reduce_sum | solution.py:12
  254.1 63.5 %all_to_all.13 = bf16[2,256,2560]{2,1,0:T(8,128)(2,1)S(1)} all-to-all(bf16[2,256,2560]{2,1,0:T(8,128)(2,1)} %bitcast.20), channel_id=1, replica_groups=mesh['row'=16,'col'=2] {'col'}, dimensions={0} | all-to-all | bytes 5242880 | tf_op jit(solution)/shard_map/all_to_all | solution.py:33
  317.6 3.0 convert_bitcast_fusion
  320.6 0.0 copy-start
  320.6 5.9 copy.9
  326.6 0.6 fusion.2
  327.2 0.0 copy-done
  327.2 3.9 fusion.4
  331.1 0.0 all-gather.7.cloned.1.call-done
  331.1 4.3 convolution_convert_fusion
  335.5 122.3 %all-gather.9.cloned.1.call-done = bf16[5120,1024]{1,0:T(8,128)(2,1)} async-done(((bf16[2560,1024]{1,0:T(8,128)(2,1)}), bf16[5120,1024]{1,0:T(8,128)(2,1)}) %all-gather.9.cloned.1.call-update) | async-done | bytes 10485776 | tf_op jit(solution)/shard_map/all_gather | solution.py:39
  457.8 7.8 %fusion.11 = f32[256,1024]{1,0:T(8,128)} fusion(bf16[256,5120]{0,1:T(8,128)(2,1)S(1)} %fusion.4, bf16[5120,1024]{1,0:T(8,128)(2,1)} %all-gather.9.cloned.1.call-done), kind=kOutput, calls=%fused_computation.16 | convolution fusion | flops 2684354560 | bytes 14155776 | tf_op jit(solution)/shard_map/dot_general | solution.py:43
  465.6 123.1 %all-gather.11.cloned.1.call-done = bf16[5120,1024]{1,0:T(8,128)(2,1)} async-done(((bf16[2560,1024]{1,0:T(8,128)(2,1)}), bf16[5120,1024]{1,0:T(8,128)(2,1)}) %all-gather.11.cloned.1.call-update) | async-done | bytes 10485776 | tf_op jit(solution)/shard_map/all_gather | solution.py:40
  588.7 8.0 %fusion.10 = bf16[256,1024]{1,0:T(8,128)(2,1)} fusion(bf16[256,5120]{0,1:T(8,128)(2,1)S(1)} %fusion.4, bf16[5120,1024]{1,0:T(8,128)(2,1)} %all-gather.11.cloned.1.call-done, f32[256,1024]{1,0:T(8,128)} %fusion.11), kind=kOutput, calls=%fused_computation.12 | convolution fusion | flops 2685927424 | bytes 14680064 | tf_op jit(solution)/shard_map/dot_general | solution.py:43
  (2 shorter events, 0.0 us)
Async XLA Ops:
  7.2 228.6 %all-gather.13.cloned.1.call-start = ((), (), s32[]{:S(2)}) async-start(), calls=%async_computation.4 | async-start | bytes 44564480 | tf_op jit(solution)/shard_map/all_gather | solution.py:11
  26.4 304.8 %all-gather.7.cloned.1.call-start = ((), (), s32[]{:S(2)}) async-start(), calls=%async_computation.1 | async-start | bytes 6881280 | tf_op jit(solution)/shard_map/all_gather | solution.py:38
  27.1 430.6 %all-gather.9.cloned.1.call-start = ((), (), s32[]{:S(2)}) async-start(), calls=%async_computation.2 | async-start | bytes 15728640 | tf_op jit(solution)/shard_map/all_gather | solution.py:39
  27.8 560.9 %all-gather.11.cloned.1.call-start = ((), (), s32[]{:S(2)}) async-start(), calls=%async_computation.3 | async-start | bytes 15728640 | tf_op jit(solution)/shard_map/all_gather | solution.py:40
  320.6 6.6 %copy-start = (f32[5120]{0:T(1024)S(1)}, f32[5120]{0:T(1024)}, u32[]{:S(2)}) copy-start(f32[5120]{0:T(1024)} %param.8) | copy-start | bytes 61444
Sparse Core Ops, SparseCore 0:
  26.5 209.2 all-gather.12
  237.3 89.2 all-gather.6
  328.2 129.5 all-gather.8
  459.2 129.5 all-gather.10
